TPU v7x, 256 devices: a whole 4x4x8 slice. The times are simulated.
256 devices in a mesh: rows: 32 (over z, x), cols: 8 (over y, core).
Axes of the slice: x: 4, y: 4, z: 8, core: 2. Of those that a mesh axis runs over, the one named last changes fastest.
Arguments:
- features: bfloat16 [524288, 440], P(('rows', 'cols')), may hold values from -12 to 12
- residual: float32 [524288, 147], P(('rows', 'cols')), may hold values from -6 to 6
- coeffs: float32 [524288, 147], P(('rows', 'cols')), may hold values from -3 to 3
- block_inverse: float32 [2, 2048, 2048], P(None, ('rows', 'cols')), may hold values from -0.0234375 to 0.0234375
- block_index: int32 [2, 2048], P(None, 'cols'), may hold values from 0 to 2047, as said below
- owners: int32 [2], replicated, may hold values from 0 to 31
Outputs:
- new_coeffs: float32 [524288, 147], P(('rows', 'cols'))
- new_residual: float32 [524288, 147], P(('rows', 'cols'))
Inputs may be any that keep to these rules, and one draw needn't show every extreme that they name: `block_index`: for each step and each aligned run of 256 positions, the indices are distinct.
All inputs are finite; a program needn't handle non-finite values.
Results may differ from a plain program's by a relative error of at most 0.0028.
Values may be sent and summed in bfloat16 or wider, within the bound.
A program may use at most 64 MiB of HBM per device.

v0:
```python
import jax
import jax.numpy as jnp
from jax import lax
from jax.sharding import Mesh
from jax.sharding import PartitionSpec as P

ROWS = ("rows_0", "rows_1")
COLS = ("cols_0", "cols_1")
ROWS_COLS = ("rows_0", "rows_1", "cols_0", "cols_1")
penalty = 0.5


def from_root(value, axes, root):
    value = jnp.where(lax.axis_index(axes) == root, value, jnp.zeros_like(value))
    for axis in axes:
        value = lax.psum(value, axis)
    return value


def in_order(parts, dim):
    shape = list(parts.shape[1:])
    shape[dim] *= parts.shape[0]
    return jnp.moveaxis(parts, 0, dim).reshape(shape)


def copy_for_each(value, axis):
    copies = jnp.broadcast_to(value, (lax.axis_size(axis), *value.shape))
    return lax.all_to_all(copies, axis, split_axis=0, concat_axis=0, tiled=True)


def collect(value, axis, dim):
    return in_order(copy_for_each(value, axis), dim)


def from_root_2(value, axis, root):
    return lax.dynamic_index_in_dim(lax.all_gather(value, axis), root, 0, keepdims=False)


def stacked_from(value, axes, order):
    parts = value[None]
    for k in order:
        parts = lax.all_gather(parts, axes[k], axis=0, tiled=True)
    block = [lax.axis_size(axes[k]) for k in reversed(order)]
    parts = parts.reshape(*block, *value.shape)
    turned = sorted(range(len(order)), key=lambda place: order[len(order) - 1 - place])
    return parts.transpose(*turned, *range(len(order), parts.ndim)).reshape(-1, *value.shape)


def gather_axes(value, axes, order, dim):
    return in_order(stacked_from(value, axes, order), dim)


def per_device(features, residual, coeffs, block_inverse, block_index, owners):
    frame_count = features.shape[0]
    feature_width = features.shape[1]
    per_col = block_index.shape[1]
    row_block = min(512, frame_count)
    exponent = -1.0 / feature_width
    my_row = lax.axis_index(ROWS)
    my_col = lax.axis_index(COLS)
    squares = jnp.sum(jnp.square(features.astype(jnp.float32)), axis=1)
    feature_blocks = features.reshape(frame_count // row_block, row_block, feature_width)
    norm_blocks = squares.reshape(frame_count // row_block, row_block)
    for step_id in range(block_index.shape[0]):
        chosen_rows = block_index[step_id]
        owner_row = owners[step_id]
        mine_feat = jnp.take(features, chosen_rows, axis=0)
        mine_res = jnp.take(residual, chosen_rows, axis=0)
        row_piece = from_root(mine_feat, ROWS, owner_row)
        chosen = collect(row_piece, COLS, 0)
        res_piece = from_root_2(mine_res, ROWS, owner_row)
        picked_res = collect(res_piece, COLS, 0)
        my_update = jnp.dot(
            block_inverse[step_id],
            picked_res,
            precision=lax.Precision.HIGHEST,
            preferred_element_type=jnp.float32,
        ).astype(jnp.bfloat16)
        update = gather_axes(my_update, ROWS_COLS, (1, 0, 2, 3), 0)
        chosen_norms = jnp.sum(jnp.square(chosen.astype(jnp.float32)), axis=1)

        def kernel_rows(operands):
            block_rows, block_norms = operands
            inner = lax.dot_general(
                block_rows, chosen, (((1,), (1,)), ((), ())), preferred_element_type=jnp.float32
            )
            distance = block_norms[:, None] + chosen_norms[None, :] - 2.0 * inner
            kernel = jnp.exp(distance * exponent).astype(jnp.bfloat16)
            return jnp.dot(kernel, update, preferred_element_type=jnp.float32)

        change = lax.map(kernel_rows, (feature_blocks, norm_blocks)).reshape(frame_count, -1)
        residual = residual - change
        is_owner = jnp.where(my_row == owner_row, 1.0, 0.0).astype(jnp.float32)
        mine_update = (
            lax.dynamic_slice_in_dim(update, my_col * per_col, per_col, 0).astype(jnp.float32)
            * is_owner
        )
        residual = residual.at[chosen_rows].add(-penalty * mine_update)
        coeffs = coeffs.at[chosen_rows].add(mine_update)
    return (coeffs, residual)


def solution(mesh):
    split = Mesh(mesh.devices.reshape(8, 4, 4, 2), ("rows_0", "rows_1", "cols_0", "cols_1"))
    in_specs = (
        P(ROWS_COLS, None),
        P(ROWS_COLS, None),
        P(ROWS_COLS, None),
        P(None, ROWS_COLS, None),
        P(None, COLS),
        P(),
    )
    out_specs = (P(ROWS_COLS, None), P(ROWS_COLS, None))
    return jax.shard_map(
        per_device, mesh=split, in_specs=in_specs, out_specs=out_specs, check_vma=False
    )
```

profile of v0, /device:TPU:1, one launch (start us, length us, event | category | flops | bytes accessed | tf_op | source)
XLA Modules:
  0.0 525.2 jit_solution(5898855721030536369)
XLA Ops:
  8.8 1.4 fusion.41
  11.5 2.8 copy.53
  14.3 1.9 gather_fusion.1
  16.2 1.9 gather_fusion.3
  18.0 1.8 select_select_fusion.1
  19.8 1.8 select_select_fusion
  21.6 72.7 %all-reduce.5.cloned.1.call-done = (bf16[256,440]{1,0:T(8,128)(2,1)}, bf16[256,440]{1,0:T(8,128)(2,1)}) async-done(((bf16[256,440]{1,0:T(8,128)(2,1)}, bf16[256,440]{1,0:T(8,128)(2,1)}), (bf16[256,440]{1,0:T(8,128)(2,1)}, bf16[256,440]{1,0:T(8,128)(2,1)})) %all-reduce.5.cloned.1.call-update) | async-done | bytes 450576 | tf_op jit(solution)/shard_map/psum | solution.py:16
  95.3 1.0 gather_fusion
  97.1 49.7 %all-reduce.7.cloned.1.call-done = (bf16[256,440]{1,0:T(8,128)(2,1)}, bf16[256,440]{1,0:T(8,128)(2,1)}) async-done(((bf16[256,440]{1,0:T(8,128)(2,1)}, bf16[256,440]{1,0:T(8,128)(2,1)}), (bf16[256,440]{1,0:T(8,128)(2,1)}, bf16[256,440]{1,0:T(8,128)(2,1)})) %all-reduce.7.cloned.1.call-update) | async-done | bytes 450576 | tf_op jit(solution)/shard_map/psum | solution.py:16
  146.7 1.1 copy.54
  147.8 1.4 broadcast_in_dim.53
  149.2 7.2 %all-to-all-start.1 = ((bf16[8,256,440]{1,2,0:T(8,128)(2,1)}), bf16[8,256,440]{1,2,0:T(8,128)(2,1)S(1)}, u32[]{:S(2)}, u32[]{:S(2)}) async-start(bf16[8,256,440]{1,2,0:T(8,128)(2,1)} %broadcast_in_dim.53), calls=%async_computation.1 | async-start | bytes 3604480 | tf_op jit(solution)/shard_map/all_to_all | solution.py:28
  158.1 40.6 %all-gather.7.cloned.1.call-done = f32[8192,147]{1,0:T(8,128)} async-done(((f32[256,147]{1,0:T(8,128)}), f32[8192,147]{1,0:T(8,128)}) %all-gather.7.cloned.1.call-update) | async-done | bytes 4816912 | tf_op jit(solution)/shard_map/all_gather | solution.py:36
  198.7 1.0 constant_dynamic-slice_fusion.3
  199.8 1.1 broadcast_in_dim.51
  200.9 5.9 %all-to-all-start = ((f32[8,256,147]{1,2,0:T(8,128)}), f32[8,256,147]{1,2,0:T(8,128)S(1)}, u32[]{:S(2)}, u32[]{:S(2)}) async-start(f32[8,256,147]{1,2,0:T(8,128)} %broadcast_in_dim.51), calls=%async_computation | async-start | bytes 2490368 | tf_op jit(solution)/shard_map/all_to_all | solution.py:28
  206.8 1.9 multiply_reduce_fusion.2
  209.1 2.7 copy.72
  211.8 12.0 %all-to-all-done = f32[8,256,147]{1,2,0:T(8,128)S(1)} async-done(((f32[8,256,147]{1,2,0:T(8,128)}), f32[8,256,147]{1,2,0:T(8,128)S(1)}, u32[]{:S(2)}, u32[]{:S(2)}) %all-to-all-start) | async-done | bytes 1204256 | tf_op jit(solution)/shard_map/all_to_all | solution.py:28
  225.1 1.1 fusion.18
  226.2 9.1 %all-gather.1 = bf16[32,147]{1,0:T(8,128)(2,1)S(1)} all-gather(bf16[8,147]{1,0:T(8,128)(2,1)S(1)} %fusion.18), channel_id=3, replica_groups=mesh['rows_0'=8,'rows_1'=4,'cols_0'=4,'cols_1'=2] {'rows_1'}, dimensions={0}, use_global_device_ids=true | all-gather | bytes 11760 | tf_op jit(solution)/shard_map/all_gather | solution.py:42
  235.3 18.3 %all_gather.39 = bf16[32,8,147]{2,1,0:T(8,128)(2,1)S(1)} all-gather(bf16[4,8,147]{2,1,0:T(8,128)(2,1)S(1)} %bitcast.119), channel_id=1, replica_groups=mesh['rows_0'=8,'rows_1'=4,'cols_0'=4,'cols_1'=2] {'rows_0'}, dimensions={0}, use_global_device_ids=true | all-gather | bytes 84672 | tf_op jit(solution)/shard_map/all_gather | solution.py:42
  253.6 9.9 %all_gather.40 = bf16[128,8,147]{2,1,0:T(8,128)(2,1)S(1)} all-gather(bf16[32,8,147]{2,1,0:T(8,128)(2,1)S(1)} %all_gather.39), channel_id=1, replica_groups=mesh['rows_0'=8,'rows_1'=4,'cols_0'=4,'cols_1'=2] {'cols_0'}, dimensions={0}, use_global_device_ids=true | all-gather | bytes 376320 | tf_op jit(solution)/shard_map/all_gather | solution.py:42
  264.0 14.9 %all_gather.41 = bf16[256,8,147]{0,1,2:T(8,128)(2,1)S(1)} all-gather(bf16[128,8,147]{0,1,2:T(8,128)(2,1)S(1)} %copy.49), channel_id=1, replica_groups=mesh['rows_0'=8,'rows_1'=4,'cols_0'=4,'cols_1'=2] {'cols_1'}, dimensions={0}, use_global_device_ids=true | all-gather | bytes 903168 | tf_op jit(solution)/shard_map/all_gather | solution.py:42
  278.9 1.0 copy.50
  280.0 1.1 copy.51
  281.9 14.0 %while.20 = (s32[]{:T(128)}, f32[4,512,147]{1,2,0:T(8,128)S(1)}, f32[4,512]{1,0:T(4,128)S(1)}, f32[2048]{0:T(1024)S(1)}, bf16[4,512,440]{2,1,0:T(8,128)(2,1)}, /...) while((s32[]{:T(128)}, f32[4,512,147]{1,2,0:T(8,128)S(1)}, f32[4,512]{1,0:T(4,128)S(1)}, ...), condition=%wide.region_6.9_spmd, body=%wide.region_5.8_spmd.sunk | while | flops 1236271104 | bytes 3996769 | solution.py:91
  282.0 3.5 fusion.59
  285.5 3.5 fusion.59
  289.0 3.5 fusion.59
  292.5 3.5 fusion.59
  296.0 1.8 copy.58
  297.8 2.5 bitcast_subtract_fusion.1
  300.3 3.3 scatter_custom_fusion.1
  303.6 1.0 gather_fusion.2
  305.5 1.4 broadcast_in_dim.56
  306.9 4.6 all-to-all-start.3
  313.6 84.1 %all-gather.9.cloned.1.call-done = f32[8192,147]{1,0:T(8,128)} async-done(((f32[256,147]{1,0:T(8,128)}), f32[8192,147]{1,0:T(8,128)}) %all-gather.9.cloned.1.call-update) | async-done | bytes 4816912 | tf_op jit(solution)/shard_map/all_gather | solution.py:36
  397.7 1.0 constant_dynamic-slice_fusion.2
  398.8 1.1 broadcast_in_dim.54
  399.9 5.8 %all-to-all-start.2 = ((f32[8,256,147]{1,2,0:T(8,128)}), f32[8,256,147]{1,2,0:T(8,128)S(1)}, u32[]{:S(2)}, u32[]{:S(2)}) async-start(f32[8,256,147]{1,2,0:T(8,128)} %broadcast_in_dim.54), calls=%async_computation.2 | async-start | bytes 2490368 | tf_op jit(solution)/shard_map/all_to_all | solution.py:28
  405.6 2.8 copy.52
  408.4 1.9 multiply_reduce_fusion
  410.3 3.8 copy.73
  414.1 5.1 scatter_custom_fusion
  419.1 3.6 all-to-all-done.2
  423.6 1.1 fusion.19
  424.7 9.1 %all-gather.3 = bf16[32,147]{1,0:T(8,128)(2,1)S(1)} all-gather(bf16[8,147]{1,0:T(8,128)(2,1)S(1)} %fusion.19), channel_id=5, replica_groups=mesh['rows_0'=8,'rows_1'=4,'cols_0'=4,'cols_1'=2] {'rows_1'}, dimensions={0}, use_global_device_ids=true | all-gather | bytes 11760 | tf_op jit(solution)/shard_map/all_gather | solution.py:42
  433.8 18.3 %all_gather.45 = bf16[32,8,147]{2,1,0:T(8,128)(2,1)S(1)} all-gather(bf16[4,8,147]{2,1,0:T(8,128)(2,1)S(1)} %bitcast.120), channel_id=1, replica_groups=mesh['rows_0'=8,'rows_1'=4,'cols_0'=4,'cols_1'=2] {'rows_0'}, dimensions={0}, use_global_device_ids=true | all-gather | bytes 84672 | tf_op jit(solution)/shard_map/all_gather | solution.py:42
  452.1 9.9 %all_gather.46 = bf16[128,8,147]{2,1,0:T(8,128)(2,1)S(1)} all-gather(bf16[32,8,147]{2,1,0:T(8,128)(2,1)S(1)} %all_gather.45), channel_id=1, replica_groups=mesh['rows_0'=8,'rows_1'=4,'cols_0'=4,'cols_1'=2] {'cols_0'}, dimensions={0}, use_global_device_ids=true | all-gather | bytes 376320 | tf_op jit(solution)/shard_map/all_gather | solution.py:42
  462.5 15.1 %all_gather.47 = bf16[256,8,147]{0,1,2:T(8,128)(2,1)} all-gather(bf16[128,8,147]{0,1,2:T(8,128)(2,1)S(1)} %copy.62), channel_id=1, replica_groups=mesh['rows_0'=8,'rows_1'=4,'cols_0'=4,'cols_1'=2] {'cols_1'}, dimensions={0}, use_global_device_ids=true | all-gather | bytes 903168 | tf_op jit(solution)/shard_map/all_gather | solution.py:42
  477.6 1.9 copy.63
  479.5 1.1 copy.64
  480.6 5.1 scatter_custom_fusion.2
  485.6 2.7 copy.70
  488.4 16.6 %while.21 = (s32[]{:T(128)}, f32[4,512,147]{1,2,0:T(8,128)S(1)}, f32[4,512]{1,0:T(4,128)S(1)}, f32[2048]{0:T(1024)S(1)}, bf16[4,512,440]{2,1,0:T(8,128)(2,1)}, /...) while((s32[]{:T(128)}, f32[4,512,147]{1,2,0:T(8,128)S(1)}, f32[4,512]{1,0:T(4,128)S(1)}, ...), condition=%wide.region_13.16_spmd, body=%wide.region_12.15_spmd.sunk | while | flops 1236271104 | bytes 3996769 | solution.py:91
  488.5 4.1 fusion.63
  492.6 4.1 fusion.63
  496.8 4.1 fusion.63
  500.9 4.1 fusion.63
  505.0 1.8 copy.69
  506.8 3.2 bitcast_subtract_fusion
  510.0 5.1 scatter_custom_fusion.3
  515.1 2.7 copy.71
  (58 shorter events, 8.4 us)
Async XLA Ops:
  8.0 86.4 %all-reduce.5.cloned.1.call-start = ((), (), s32[]{:S(2)}) async-start(), calls=%async_computation.6 | async-start | bytes 1048576 | tf_op jit(solution)/shard_map/psum | solution.py:16
  14.3 3.7 copy-start.1
  16.2 78.3 %copy-start.3 = (f32[2048,147]{0,1:T(8,128)S(1)}, f32[2048,147]{0,1:T(8,128)}, u32[]{:S(2)}) copy-start(f32[2048,147]{0,1:T(8,128)} %param.15) | copy-start | bytes 3612676
  21.6 125.2 %all-reduce.7.cloned.1.call-start = ((), (), s32[]{:S(2)}) async-start(), calls=%async_computation.7 | async-start | bytes 1048576 | tf_op jit(solution)/shard_map/psum | solution.py:16
  94.4 104.3 %all-gather.7.cloned.1.call-start = ((), (), s32[]{:S(2)}) async-start(), calls=%async_computation.4 | async-start | bytes 8650752 | tf_op jit(solution)/shard_map/all_gather | solution.py:36
  95.3 53.9 %copy-start = (f32[2048,147]{1,0:T(8,128)}, f32[2048,147]{1,0:T(8,128)S(1)}, u32[]{:S(2)}) copy-start(f32[2048,147]{1,0:T(8,128)S(1)} %copy.46) | copy-start | bytes 3612676
  149.2 50.6 %all-to-all-start.1 = ((bf16[8,256,440]{1,2,0:T(8,128)(2,1)}), bf16[8,256,440]{1,2,0:T(8,128)(2,1)S(1)}, u32[]{:S(2)}, u32[]{:S(2)}) async-start(bf16[8,256,440]{1,2,0:T(8,128)(2,1)} %broadcast_in_dim.53), calls=%async_computation.1 | async-start | bytes 3604480 | tf_op jit(solution)/shard_map/all_to_all | solution.py:28
  200.9 7.8 %copy-start.6 = (s32[2,256]{1,0:T(2,128)S(1)}, s32[2,256]{1,0:T(2,128)}, u32[]{:S(2)}) copy-start(s32[2,256]{1,0:T(2,128)} %param.18) | copy-start | bytes 6148
  200.9 23.0 %all-to-all-start = ((f32[8,256,147]{1,2,0:T(8,128)}), f32[8,256,147]{1,2,0:T(8,128)S(1)}, u32[]{:S(2)}, u32[]{:S(2)}) async-start(f32[8,256,147]{1,2,0:T(8,128)} %broadcast_in_dim.51), calls=%async_computation | async-start | bytes 2490368 | tf_op jit(solution)/shard_map/all_to_all | solution.py:28
  206.8 190.9 %all-gather.9.cloned.1.call-start = ((), (), s32[]{:S(2)}) async-start(), calls=%async_computation.5 | async-start | bytes 8650752 | tf_op jit(solution)/shard_map/all_gather | solution.py:36
  224.2 0.9 copy-start.5
  280.0 2.0 copy-start.2
  303.6 1.8 copy-start.4
  306.9 91.8 %all-to-all-start.3 = ((bf16[8,256,440]{1,2,0:T(8,128)(2,1)}), bf16[8,256,440]{1,2,0:T(8,128)(2,1)}, u32[]{:S(2)}, u32[]{:S(2)}) async-start(bf16[8,256,440]{1,2,0:T(8,128)(2,1)} %broadcast_in_dim.56), calls=%async_computation.3 | async-start | bytes 3604480 | tf_op jit(solution)/shard_map/all_to_all | solution.py:28
  399.9 22.8 %all-to-all-start.2 = ((f32[8,256,147]{1,2,0:T(8,128)}), f32[8,256,147]{1,2,0:T(8,128)S(1)}, u32[]{:S(2)}, u32[]{:S(2)}) async-start(f32[8,256,147]{1,2,0:T(8,128)} %broadcast_in_dim.54), calls=%async_computation.2 | async-start | bytes 2490368 | tf_op jit(solution)/shard_map/all_to_all | solution.py:28
Sparse Core Ops, SparseCore 0:
  21.7 72.6 all-reduce.4
  96.8 49.8 all-reduce.6
Sparse Core Ops, SparseCore 1:
  98.0 100.6 all-gather.6
  305.5 92.2 all-gather.8
where the time goes:
time: 527 us; the launch traced here: 525 us
  waiting for transfers between devices  263 us (50%)
  blocking collectives  105 us (20%)
  local copies, waits for them, and re-layouts  47.4 us (9%)
  other arithmetic  33.4 us (6%)
  matrix products  32.5 us (6%)
  starting transfers between devices  23.5 us (4%)
  between operations  20.9 us (4%)
    all_gather x2, waiting for transfers between devices, from_root_2(): lax.all_gather(value, axis)  125 us
    psum x2, waiting for transfers between devices, from_root(): value = lax.psum(value, axis)  122 us
    all_gather x8, blocking collectives, stacked_from(): parts = lax.all_gather(parts, axes[k], axis=0, tiled=True)  105 us
    dot_general x8, matrix products, kernel_rows(): return jnp.dot(kernel, update, preferred_element_type=jnp.float32)  30.4 us
    all_to_all x4, starting transfers between devices, copy_for_each(): return lax.all_to_all(copies, axis, split_axis=0, concat_axis=0, tiled=True)  23.4 us
    all_to_all x4, waiting for transfers between devices, copy_for_each(): return lax.all_to_all(copies, axis, split_axis=0, concat_axis=0, tiled=True)  15.6 us
    unnamed x27, local copies, waits for them, and re-layouts  14.1 us
  transfers between devices with their start and end apart: 8, of which 6 were waited for; matrix products, arithmetic and copies ran while one was open for 5% of the time, Pallas kernels for 0%

commit v1 on v0

--- a/solution.py
+++ b/solution.py
@@ -39,7 +39,9 @@
 def stacked_from(value, axes, order):
     parts = value[None]
     for k in order:
-        parts = lax.all_gather(parts, axes[k], axis=0, tiled=True)
+        parts = jnp.concatenate(
+            lax.all_to_all(jnp.stack([parts] * lax.axis_size(axes[k])), axes[k], 0, 0), axis=0
+        )
     block = [lax.axis_size(axes[k]) for k in reversed(order)]
     parts = parts.reshape(*block, *value.shape)
     turned = sorted(range(len(order)), key=lambda place: order[len(order) - 1 - place])

time: 527 us -> 589 us (1.12)
  waiting for transfers between devices: 263 us -> 361 us
  blocking collectives: 105 us -> 44 us
  starting transfers between devices: 23.5 us -> 37.4 us
  local copies, waits for them, and re-layouts: 47.4 us -> 58.7 us
    all_gather x8 -> x0, blocking collectives: 105 us -> none  [stacked_from(): parts = lax.all_gather(parts, axes[k], axis=0, tiled=True)]
    all_gather x2, waiting for transfers between devices: 125 us -> 174 us  [from_root_2(): lax.all_gather(value, axis)]
    all_to_all x0 -> x5, blocking collectives: none -> 44 us  [stacked_from(): lax.all_to_all(jnp.stack([parts] * lax.axis_size(axes[k])), axes[k], 0, 0)]
    all_to_all x4, waiting for transfers between devices: 15.6 us -> 57.2 us  [copy_for_each(): return lax.all_to_all(copies, axis, split_axis=0, concat_axis=0, tiled=True)]
    all_to_all x0 -> x3, starting transfers between devices: none -> 13.7 us  [stacked_from(): lax.all_to_all(jnp.stack([parts] * lax.axis_size(axes[k])), axes[k], 0, 0)]
    all_to_all x0 -> x3, waiting for transfers between devices: none -> 9.7 us  [stacked_from(): lax.all_to_all(jnp.stack([parts] * lax.axis_size(axes[k])), axes[k], 0, 0)]
    unnamed x27 -> x25, local copies, waits for them, and re-layouts: 14.1 us -> 16.9 us
  transfers between devices with their start and end apart: 8 -> 11, of which waited for: 6 -> 9; matrix products, arithmetic and copies ran while one was open for 5% -> 6% of each run, Pallas kernels for 0% -> 0%
where the time goes in v1:
time: 589 us; the launch traced here: 587 us
  waiting for transfers between devices  361 us (61%)
  local copies, waits for them, and re-layouts  58.7 us (10%)
  blocking collectives  44 us (7%)
  starting transfers between devices  37.4 us (6%)
  other arithmetic  33.1 us (6%)
  matrix products  32.5 us (6%)
  between operations  20.7 us (4%)
    all_gather x2, waiting for transfers between devices, from_root_2(): lax.all_gather(value, axis)  174 us
    psum x2, waiting for transfers between devices, from_root(): value = lax.psum(value, axis)  120 us
    all_to_all x4, waiting for transfers between devices, copy_for_each(): return lax.all_to_all(copies, axis, split_axis=0, concat_axis=0, tiled=True)  57.2 us
    all_to_all x5, blocking collectives, stacked_from(): lax.all_to_all(jnp.stack([parts] * lax.axis_size(axes[k])), axes[k], 0, 0)  44 us
    dot_general x8, matrix products, kernel_rows(): return jnp.dot(kernel, update, preferred_element_type=jnp.float32)  30.4 us
    all_to_all x4, starting transfers between devices, copy_for_each(): return lax.all_to_all(copies, axis, split_axis=0, concat_axis=0, tiled=True)  23.6 us
    unnamed x25, local copies, waits for them, and re-layouts  16.9 us
    all_to_all x3, starting transfers between devices, stacked_from(): lax.all_to_all(jnp.stack([parts] * lax.axis_size(axes[k])), axes[k], 0, 0)  13.7 us
  transfers between devices with their start and end apart: 11, of which 9 were waited for; matrix products, arithmetic and copies ran while one was open for 6% of the time, Pallas kernels for 0%

profile of v1, /device:TPU:1, one launch (start us, length us, event | category | flops | bytes accessed | tf_op | source)
XLA Modules:
  0.0 587.3 jit_solution(11105863402617033714)
XLA Ops:
  8.8 1.8 copy.46
  15.6 3.8 copy.53
  19.4 3.1 gather_fusion.1
  22.5 3.1 gather_fusion.3
  27.0 86.5 %all-gather.5.cloned.1.call-done = f32[8192,147]{1,0:T(8,128)} async-done(((f32[256,147]{1,0:T(8,128)}), f32[8192,147]{1,0:T(8,128)}) %all-gather.5.cloned.1.call-update) | async-done | bytes 4816912 | tf_op jit(solution)/shard_map/all_gather | solution.py:36
  114.6 1.1 broadcast_in_dim.45
  115.7 5.7 all-to-all-start
  122.3 68.2 %all-reduce.5.cloned.1.call-done = (bf16[256,440]{1,0:T(8,128)(2,1)}, bf16[256,440]{1,0:T(8,128)(2,1)}) async-done(((bf16[256,440]{1,0:T(8,128)(2,1)}, bf16[256,440]{1,0:T(8,128)(2,1)}), (bf16[256,440]{1,0:T(8,128)(2,1)}, bf16[256,440]{1,0:T(8,128)(2,1)})) %all-reduce.5.cloned.1.call-update) | async-done | bytes 450576 | tf_op jit(solution)/shard_map/psum | solution.py:16
  190.5 51.6 %all-reduce.7.cloned.1.call-done = (bf16[256,440]{1,0:T(8,128)(2,1)}, bf16[256,440]{1,0:T(8,128)(2,1)}) async-done(((bf16[256,440]{1,0:T(8,128)(2,1)}, bf16[256,440]{1,0:T(8,128)(2,1)}), (bf16[256,440]{1,0:T(8,128)(2,1)}, bf16[256,440]{1,0:T(8,128)(2,1)})) %all-reduce.7.cloned.1.call-update) | async-done | bytes 450576 | tf_op jit(solution)/shard_map/psum | solution.py:16
  242.1 1.1 copy.54
  243.2 1.4 broadcast_in_dim.46
  244.5 7.0 %all-to-all-start.5 = ((bf16[8,256,440]{1,2,0:T(8,128)(2,1)}), bf16[8,256,440]{1,2,0:T(8,128)(2,1)S(1)}, u32[]{:S(2)}, u32[]{:S(2)}) async-start(bf16[8,256,440]{1,2,0:T(8,128)(2,1)} %broadcast_in_dim.46), calls=%async_computation.5 | async-start | bytes 3604480 | tf_op jit(solution)/shard_map/all_to_all | solution.py:28
  252.9 1.1 fusion.18
  254.0 20.7 %all-to-all-done.5 = bf16[8,256,440]{1,2,0:T(8,128)(2,1)S(1)} async-done(((bf16[8,256,440]{1,2,0:T(8,128)(2,1)}), bf16[8,256,440]{1,2,0:T(8,128)(2,1)S(1)}, u32[]{:S(2)}, u32[]{:S(2)}) %all-to-all-start.5) | async-done | bytes 1802272 | tf_op jit(solution)/shard_map/all_to_all | solution.py:28
  274.6 7.2 %all_to_all.60 = bf16[4,1,8,147]{3,2,1,0:T(8,128)(2,1)S(1)} all-to-all(bf16[4,1,8,147]{3,2,1,0:T(8,128)(2,1)S(1)} %stack.24), channel_id=1, replica_groups=mesh['rows_0'=8,'rows_1'=4,'cols_0'=4,'cols_1'=2] {'rows_1'}, dimensions={0} | all-to-all | bytes 18816 | tf_op jit(solution)/shard_map/all_to_all | solution.py:43
  282.5 6.7 %all-to-all-start.2 = ((bf16[8,4,8,147]{3,2,1,0:T(8,128)(2,1)}), bf16[8,4,8,147]{3,2,1,0:T(8,128)(2,1)S(1)}, u32[]{:S(2)}, u32[]{:S(2)}) async-start(bf16[8,4,8,147]{3,2,1,0:T(8,128)(2,1)} %stack.25), calls=%async_computation.2 | async-start | bytes 262144 | tf_op jit(solution)/shard_map/all_to_all | solution.py:43
  289.2 7.9 %all-to-all-done.2 = bf16[8,4,8,147]{3,2,1,0:T(8,128)(2,1)S(1)} async-done(((bf16[8,4,8,147]{3,2,1,0:T(8,128)(2,1)}), bf16[8,4,8,147]{3,2,1,0:T(8,128)(2,1)S(1)}, u32[]{:S(2)}, u32[]{:S(2)}) %all-to-all-start.2) | async-done | bytes 75296 | tf_op jit(solution)/shard_map/all_to_all | solution.py:43
  298.0 3.5 all-to-all-start.3
  301.5 1.9 multiply_reduce_fusion.2
  303.8 2.8 copy.72
  306.5 1.8 all-to-all-done.3
  308.5 1.2 copy.49
  309.7 8.9 %all_to_all.61 = bf16[2,128,8,147]{1,2,3,0:T(8,128)(2,1)S(1)} all-to-all(bf16[2,128,8,147]{1,2,3,0:T(8,128)(2,1)S(1)} %copy.49), channel_id=1, replica_groups=mesh['rows_0'=8,'rows_1'=4,'cols_0'=4,'cols_1'=2] {'cols_1'}, dimensions={0} | all-to-all | bytes 1204224 | tf_op jit(solution)/shard_map/all_to_all | solution.py:43
  319.5 1.1 copy.51
  321.5 14.0 %while.20 = (s32[]{:T(128)}, f32[4,512,147]{1,2,0:T(8,128)S(1)}, f32[4,512]{1,0:T(4,128)S(1)}, f32[2048]{0:T(1024)S(1)}, bf16[4,512,440]{2,1,0:T(8,128)(2,1)}, /...) while((s32[]{:T(128)}, f32[4,512,147]{1,2,0:T(8,128)S(1)}, f32[4,512]{1,0:T(4,128)S(1)}, ...), condition=%wide.region_6.9_spmd, body=%wide.region_5.8_spmd.sunk | while | flops 1236271104 | bytes 3996769 | solution.py:93
  321.5 3.5 fusion.59
  325.0 3.5 fusion.59
  328.5 3.5 fusion.59
  332.0 3.5 fusion.59
  335.5 1.8 copy.58
  337.3 2.5 bitcast_subtract_fusion.1
  339.8 3.1 scatter_custom_fusion.1
  346.5 87.6 %all-gather.7.cloned.1.call-done = f32[8192,147]{1,0:T(8,128)} async-done(((f32[256,147]{1,0:T(8,128)}), f32[8192,147]{1,0:T(8,128)}) %all-gather.7.cloned.1.call-update) | async-done | bytes 4816912 | tf_op jit(solution)/shard_map/all_gather | solution.py:36
  435.2 1.1 broadcast_in_dim.47
  436.3 5.7 all-to-all-start.6
  442.0 1.8 copy.66
  443.8 15.3 %all-to-all-done.6 = f32[8,256,147]{1,2,0:T(8,128)S(1)} async-done(((f32[8,256,147]{1,2,0:T(8,128)}), f32[8,256,147]{1,2,0:T(8,128)S(1)}, u32[]{:S(2)}, u32[]{:S(2)}) %all-to-all-start.6) | async-done | bytes 1204256 | tf_op jit(solution)/shard_map/all_to_all | solution.py:28
  459.1 2.3 broadcast_in_dim.48
  461.3 5.2 all-to-all-start.11
  467.4 1.1 fusion.19
  468.5 21.2 %all-to-all-done.11 = bf16[8,256,440]{1,2,0:T(8,128)(2,1)} async-done(((bf16[8,256,440]{1,2,0:T(8,128)(2,1)}), bf16[8,256,440]{1,2,0:T(8,128)(2,1)}, u32[]{:S(2)}, u32[]{:S(2)}) %all-to-all-start.11) | async-done | bytes 1802272 | tf_op jit(solution)/shard_map/all_to_all | solution.py:28
  489.7 6.5 %all_to_all.62 = bf16[4,1,8,147]{3,2,1,0:T(8,128)(2,1)S(1)} all-to-all(bf16[4,1,8,147]{3,2,1,0:T(8,128)(2,1)S(1)} %stack.28), channel_id=1, replica_groups=mesh['rows_0'=8,'rows_1'=4,'cols_0'=4,'cols_1'=2] {'rows_1'}, dimensions={0} | all-to-all | bytes 18816 | tf_op jit(solution)/shard_map/all_to_all | solution.py:43
  496.2 11.8 %all_to_all.63 = bf16[8,4,8,147]{3,2,1,0:T(8,128)(2,1)S(1)} all-to-all(bf16[8,4,8,147]{3,2,1,0:T(8,128)(2,1)S(1)} %stack.29), channel_id=1, replica_groups=mesh['rows_0'=8,'rows_1'=4,'cols_0'=4,'cols_1'=2] {'rows_0'}, dimensions={0} | all-to-all | bytes 150528 | tf_op jit(solution)/shard_map/all_to_all | solution.py:43
  508.9 3.5 all-to-all-start.9
  512.4 2.8 copy.52
  515.1 1.9 multiply_reduce_fusion
  517.0 3.8 copy.73
  520.9 5.1 scatter_custom_fusion
  526.7 1.5 pad_maximum_fusion.1
  528.2 1.8 copy.62
  530.0 9.6 %all_to_all.64 = bf16[2,128,8,147]{1,2,3,0:T(8,128)(2,1)} all-to-all(bf16[2,128,8,147]{1,2,3,0:T(8,128)(2,1)} %copy.62), channel_id=1, replica_groups=mesh['rows_0'=8,'rows_1'=4,'cols_0'=4,'cols_1'=2] {'cols_1'}, dimensions={0} | all-to-all | bytes 1204224 | tf_op jit(solution)/shard_map/all_to_all | solution.py:43
  539.6 1.9 copy.63
  541.5 1.1 copy.64
  542.6 5.1 scatter_custom_fusion.2
  547.7 2.7 copy.70
  550.5 16.6 %while.21 = (s32[]{:T(128)}, f32[4,512,147]{1,2,0:T(8,128)S(1)}, f32[4,512]{1,0:T(4,128)S(1)}, f32[2048]{0:T(1024)S(1)}, bf16[4,512,440]{2,1,0:T(8,128)(2,1)}, /...) while((s32[]{:T(128)}, f32[4,512,147]{1,2,0:T(8,128)S(1)}, f32[4,512]{1,0:T(4,128)S(1)}, ...), condition=%wide.region_13.16_spmd, body=%wide.region_12.15_spmd.sunk | while | flops 1236271104 | bytes 3996769 | solution.py:93
  550.5 4.1 fusion.63
  554.7 4.1 fusion.63
  558.8 4.1 fusion.63
  563.0 4.1 fusion.63
  567.1 1.8 copy.69
  568.9 3.2 bitcast_subtract_fusion
  572.1 5.1 scatter_custom_fusion.3
  577.2 2.7 copy.71
  (67 shorter events, 16.8 us)
Async XLA Ops:
  8.0 105.5 %all-gather.5.cloned.1.call-start = ((), (), s32[]{:S(2)}) async-start(), calls=%async_computation.12 | async-start | bytes 8650752 | tf_op jit(solution)/shard_map/all_gather | solution.py:36
  10.6 8.8 %copy-start = (f32[2048,147]{1,0:T(8,128)}, f32[2048,147]{1,0:T(8,128)S(1)}, u32[]{:S(2)}) copy-start(f32[2048,147]{1,0:T(8,128)S(1)} %copy.46) | copy-start | bytes 3612676
  10.6 1.8 copy-start.5
  115.7 127.5 %all-to-all-start = ((f32[8,256,147]{1,2,0:T(8,128)}), f32[8,256,147]{1,2,0:T(8,128)S(1)}, u32[]{:S(2)}, u32[]{:S(2)}) async-start(f32[8,256,147]{1,2,0:T(8,128)} %broadcast_in_dim.45), calls=%async_computation | async-start | bytes 2490368 | tf_op jit(solution)/shard_map/all_to_all | solution.py:28
  121.4 69.1 %all-reduce.5.cloned.1.call-start = ((), (), s32[]{:S(2)}) async-start(), calls=%async_computation.14 | async-start | bytes 1048576 | tf_op jit(solution)/shard_map/psum | solution.py:16
  122.2 119.8 %all-reduce.7.cloned.1.call-start = ((), (), s32[]{:S(2)}) async-start(), calls=%async_computation.15 | async-start | bytes 1048576 | tf_op jit(solution)/shard_map/psum | solution.py:16
  244.5 30.1 %all-to-all-start.5 = ((bf16[8,256,440]{1,2,0:T(8,128)(2,1)}), bf16[8,256,440]{1,2,0:T(8,128)(2,1)S(1)}, u32[]{:S(2)}, u32[]{:S(2)}) async-start(bf16[8,256,440]{1,2,0:T(8,128)(2,1)} %broadcast_in_dim.46), calls=%async_computation.5 | async-start | bytes 3604480 | tf_op jit(solution)/shard_map/all_to_all | solution.py:28
  252.0 0.9 copy-start.3
  252.1 37.1 %copy-start.4 = (s32[2,256]{1,0:T(2,128)S(1)}, s32[2,256]{1,0:T(2,128)}, u32[]{:S(2)}) copy-start(s32[2,256]{1,0:T(2,128)} %param.18) | copy-start | bytes 6148
  282.5 14.7 %all-to-all-start.2 = ((bf16[8,4,8,147]{3,2,1,0:T(8,128)(2,1)}), bf16[8,4,8,147]{3,2,1,0:T(8,128)(2,1)S(1)}, u32[]{:S(2)}, u32[]{:S(2)}) async-start(bf16[8,4,8,147]{3,2,1,0:T(8,128)(2,1)} %stack.25), calls=%async_computation.2 | async-start | bytes 262144 | tf_op jit(solution)/shard_map/all_to_all | solution.py:43
  298.0 10.4 %all-to-all-start.3 = ((bf16[4,32,8,147]{3,2,1,0:T(8,128)(2,1)}), bf16[4,32,8,147]{3,2,1,0:T(8,128)(2,1)S(1)}, u32[]{:S(2)}, u32[]{:S(2)}) async-start(bf16[4,32,8,147]{3,2,1,0:T(8,128)(2,1)} %stack.26), calls=%async_computation.3 | async-start | bytes 1048576 | tf_op jit(solution)/shard_map/all_to_all | solution.py:43
  301.4 132.7 %all-gather.7.cloned.1.call-start = ((), (), s32[]{:S(2)}) async-start(), calls=%async_computation.13 | async-start | bytes 8650752 | tf_op jit(solution)/shard_map/all_gather | solution.py:36
  319.5 2.0 copy-start.2
  436.3 22.8 %all-to-all-start.6 = ((f32[8,256,147]{1,2,0:T(8,128)}), f32[8,256,147]{1,2,0:T(8,128)S(1)}, u32[]{:S(2)}, u32[]{:S(2)}) async-start(f32[8,256,147]{1,2,0:T(8,128)} %broadcast_in_dim.47), calls=%async_computation.6 | async-start | bytes 2490368 | tf_op jit(solution)/shard_map/all_to_all | solution.py:28
  461.3 28.4 %all-to-all-start.11 = ((bf16[8,256,440]{1,2,0:T(8,128)(2,1)}), bf16[8,256,440]{1,2,0:T(8,128)(2,1)}, u32[]{:S(2)}, u32[]{:S(2)}) async-start(bf16[8,256,440]{1,2,0:T(8,128)(2,1)} %broadcast_in_dim.48), calls=%async_computation.11 | async-start | bytes 3604480 | tf_op jit(solution)/shard_map/all_to_all | solution.py:28
  508.9 17.0 %all-to-all-start.9 = ((bf16[4,32,8,147]{3,2,1,0:T(8,128)(2,1)}), bf16[4,32,8,147]{3,2,1,0:T(8,128)(2,1)S(1)}, u32[]{:S(2)}, u32[]{:S(2)}) async-start(bf16[4,32,8,147]{3,2,1,0:T(8,128)(2,1)} %stack.30), calls=%async_computation.9 | async-start | bytes 1048576 | tf_op jit(solution)/shard_map/all_to_all | solution.py:43
  525.9 0.8 copy-start.1
Sparse Core Ops, SparseCore 0:
  12.6 100.8 all-gather.4
  344.9 89.1 all-gather.6
Sparse Core Ops, SparseCore 1:
  124.8 65.6 all-reduce.4
  192.7 49.3 all-reduce.6
